TPU v7x, 128 devices: a whole 4x4x4 slice. The times are simulated.
128 devices in a mesh: queue: 32 (over y, x, z_lo), head: 4 (over z_hi, core).
Axes of the slice: x: 4, y: 4, z: 4 (z_hi: 2, z_lo: 2; z = z_hi * 2 + z_lo), core: 2. Of those that a mesh axis runs over, the one named last changes fastest.
Arguments:
- latents: bfloat16 [64, 384, 5120], P('queue'), may hold values from -6 to 6
- control: bfloat16 [64, 384, 5120], P('queue'), may hold values from -3 to 3
- levels: int32 [64], P('queue'), may hold values from 0 to 63
- window_mask: int32 [64, 2], P('queue'), may hold values 0 or 1
- modulation: float32 [64, 3, 5120], replicated, may hold values from -3 to 3
- w_query: bfloat16 [5120, 2560], P('queue', 'head'), may hold values from -1 to 1
- w_key: bfloat16 [5120, 2560], P('queue', 'head'), may hold values from -1 to 1
- w_value: bfloat16 [5120, 2560], P('queue', 'head'), may hold values from -0.078125 to 0.078125
- w_out: bfloat16 [2560, 5120], P('head', 'queue'), may hold values from -0.125 to 0.125
- q_gain: float32 [2560], P('head'), may hold values from 0.6 to 8
- k_gain: float32 [2560], P('head'), may hold values from 0.6 to 8
Outputs:
- next_queue: float32 [64, 384, 5120], P('queue', None, 'head')
All inputs are finite; a program needn't handle non-finite values. No bound on the sum of `window_mask` on one device may be relied on, other than what follows from the above.
Results may differ from a plain program's by a relative error of at most 0.019.
The roundings to bfloat16 on the way count: a program that leaves them out, or rounds other values in their place, can miss the bound.
Values may be sent and summed in bfloat16 or wider, within the bound.
A program may use at most 192 MiB of HBM per device.

v0:
```python
import functools

import jax
import jax.numpy as jnp
from jax import lax
from jax.experimental import pallas as pl
from jax.experimental.pallas import tpu as pltpu
from jax.sharding import PartitionSpec as P

HD = 128
MESH = pl.DeviceIdType.MESH
BF = jnp.bfloat16
F32 = jnp.float32
XCS = (384, 256, 384)
TILE = 192
LNB = 64


def place(x, y, z, c):
    x, y, z = x % 4, y % 4, z % 4
    return ((y * 4 + x) * 2 + z % 2, (z // 2) * 2 + c)


def where_am_i():
    q = lax.axis_index("queue")
    h = lax.axis_index("head")
    return (q // 2) % 4, q // 8, (h // 2) * 2 + q % 2, h % 2


def remote(src, dst, ss, rs, dev):
    return pltpu.make_async_remote_copy(
        src_ref=src, dst_ref=dst, send_sem=ss, recv_sem=rs, device_id=dev, device_id_type=MESH
    )


def block_kernel(
    lat, ctl, mods, wk, wv, wq, bias, wo,
    out, shin,
    W, N, lstage, cstage, acc, sq, sqr, qo, ko, vo, pko, pvo, biaso, WO, AT, shout, EX,
    stsem, plsem, plrsem, asem, arsem, bsem, brsem, fsem, frsem,
    xsem, xrsem, ssem, srsem, ksem, krsem, bisem, birsem,
    rsem, rrsem, wasem, warsem, wbsem, wbrsem, tsem, trsem, gsem, grsem, lsem, hsem, hrsem, osem,
):
    x, y, z, c = where_am_i()
    zl = z % 2
    zh = z // 2
    mine = place(x, y, z, c)
    partner = place(x, y, z, 1 - c)
    swapped = c != zl
    p = y * 4 + x
    pn = (p + 1) % 16
    pp = (p + 15) % 16
    nxt = place(pn % 4, pn // 4, z, 1 - c)
    prv = place(pp % 4, pp // 4, z, 1 - c)

    q = lax.axis_index("queue")
    h = lax.axis_index("head")
    after = ((q + 1) % 32, h)
    before = ((q + 31) % 32, h)
    barrier = pltpu.get_barrier_semaphore()

    def swapdev(t):
        return ((h * 4 + x) * 2 + t, y)


    def greet(dev):
        pl.semaphore_signal(barrier, inc=1, device_id=dev, device_id_type=MESH)

    for d in (1, 2, 3):
        greet(place(x + d, y, z, c))
        greet(place(x, y + d, z, c))
        greet(place(x, y, z + d, c))
    greet(partner)

    @pl.when(c == 1)
    def _():
        greet(nxt)

    @pl.when(c == 0)
    def _():
        greet(prv)

    @pl.when(swapped)
    def _():
        greet(place(x, y, z + 1, 1 - c))
        greet(place(x, y, z + 3, 1 - c))

    @pl.when(y != h)
    def _():
        greet(swapdev(0))
        greet(swapdev(1))

    @pl.when(y == h)
    def _():
        greet(swapdev(1 - zl))

    greet(after)
    greet(before)
    pl.semaphore_wait(barrier, jnp.where(swapped, 13, 11) + jnp.where(y != h, 2, 1) + 2)

    swap_dev = place(x, y, 2 * zh + c, 1 - c)
    ws = (wk, wv, wq)

    def slot(m):
        return W.at[m, y, x, zl]

    @pl.when(swapped)
    def _():
        for m in range(3):
            remote(ws[m], slot(m), plsem.at[m], plrsem.at[m], swap_dev).start()
        remote(bias, biaso, bisem, birsem, swap_dev).start()

    @pl.when(jnp.logical_not(swapped))
    def _():
        for m in range(3):
            pltpu.make_async_copy(ws[m], slot(m), plsem.at[m]).start()
        pltpu.make_async_copy(bias, biaso, bisem).start()

    n_chunks = jnp.where(swapped, 384 // LNB, 768 // LNB)
    row0 = jnp.where(swapped, zh * 384, 0)
    out0 = jnp.where(swapped, 768, 0)

    def stage(i, s):
        r = pl.multiple_of(row0 + i * LNB, LNB)
        return (
            pltpu.make_async_copy(lat.at[pl.ds(r, LNB)], lstage.at[s], stsem.at[0, s]),
            pltpu.make_async_copy(ctl.at[pl.ds(r, LNB)], cstage.at[s], stsem.at[1, s]),
        )

    for cp in stage(0, 0):
        cp.start()

    def piece(m, half, d, part):
        rows = slice(None) if part is None else pl.ds(part * 80, 80)
        if half == 0:
            return W.at[m, y, (x + 4 - d) % 4, c, rows, pl.ds(0, XCS[m])]
        return W.at[m, (y + 4 - d) % 4, x, c, rows, pl.ds(XCS[m], 640 - XCS[m])]

    def chunk(m, half, d, part=None):
        many = slice(None) if part is None else pl.ds(part * 2, 2)
        if half == 0:
            return W.at[m, (y + 4 - d) % 4, many, c, :, pl.ds(0, XCS[m])]
        return W.at[m, many, (x + 4 - d) % 4, c, :, pl.ds(XCS[m], 640 - XCS[m])]

    def along(axis, way):
        d = 1 if way == 0 else 3
        return place(x + d, y, z, c) if axis == 0 else place(x, y + d, z, c)

    def a_copy(m, half, way, part):
        ref = piece(m, half, 0, part)
        return remote(ref, ref, asem.at[m, half, way, part], arsem.at[m, half, way, part], along(half, way))

    def a_relay(m, half, way):
        ref = piece(m, half, 1 if way == 0 else 3, way)
        return remote(ref, ref, asem.at[m, half, way, 2], arsem.at[m, half, way, 2], along(half, way))

    def b_copy(m, half, way, part):
        ref = chunk(m, half, 0, part)
        return remote(ref, ref, bsem.at[m, half, way, part], brsem.at[m, half, way, part], along(1 - half, way))

    def b_relay(m, half, way):
        ref = chunk(m, half, 1 if way == 0 else 3, way)
        return remote(ref, ref, bsem.at[m, half, way, 2], brsem.at[m, half, way, 2], along(1 - half, way))

    def f_copy(m, half, d):
        ref = chunk(m, half, d)
        return remote(ref, ref, fsem.at[m, half, d], frsem.at[m, half, d], partner)

    def step_a1(m):
        @pl.when(swapped)
        def _():
            remote(ws[m], W.at[m, y, x, c], plsem.at[m], plrsem.at[m], swap_dev).wait()

        @pl.when(jnp.logical_not(swapped))
        def _():
            pltpu.make_async_copy(ws[m], slot(m), plsem.at[m]).wait()

        for part in (0, 1):
            for way in (0, 1):
                for half in (0, 1):
                    a_copy(m, half, way, part ^ way).start()

    def step_a2(m):
        for way in (0, 1):
            for half in (0, 1):
                a_copy(m, half, way, way).wait_recv()
                a_relay(m, half, way).start()

    def step_b1(m):
        for half in (0, 1):
            for way in (0, 1):
                a_copy(m, half, way, 1 - way).wait_recv()
                a_relay(m, half, way).wait_recv()
        for part in (0, 1):
            for way in (0, 1):
                for half in (0, 1):
                    b_copy(m, half, way, part ^ way).start()
        for half in (0, 1):
            f_copy(m, half, 0).start()

    def step_b2(m):
        for way in (0, 1):
            for half in (0, 1):
                b_copy(m, half, way, way).wait_recv()
                b_relay(m, half, way).start()

    def step_f(m):
        for half in (0, 1):
            for way in (0, 1):
                b_copy(m, half, way, 1 - way).wait_recv()
                f_copy(m, half, 1 if way == 0 else 3).start()

    def step_f2(m):
        for half in (0, 1):
            for way in (0, 1):
                b_relay(m, half, way).wait_recv()
            f_copy(m, half, 2).start()

    spot = WO.at[h, x, zl]

    def w_place():
        @pl.when(y != h)
        def _():
            for t in (0, 1):
                remote(wo, spot, rsem.at[t], rrsem.at[zl], swapdev(t)).start()

        @pl.when(y == h)
        def _():
            pltpu.make_async_copy(wo, spot, lsem.at[0]).start()
            remote(wo, spot, rsem.at[0], rrsem.at[zl], swapdev(1 - zl)).start()

    def w_placed():
        @pl.when(y != h)
        def _():
            for t in (0, 1):
                remote(wo, WO.at[y, x, t], rsem.at[t], rrsem.at[t], partner).wait_recv()

        @pl.when(y == h)
        def _():
            pltpu.make_async_copy(wo, spot, lsem.at[0]).wait()
            remote(wo, spot, rsem.at[0], rrsem.at[1 - zl], partner).wait_recv()

    def w_piece(half, d, part):
        rows = pl.ds(part * 80, 80)
        if half == 0:
            return WO.at[y, (x + 4 - d) % 4, 0, rows]
        return WO.at[(y + 4 - d) % 4, x, 1, rows]

    def w_chunk(half, d, part):
        many = pl.ds(part * 2, 2)
        if half == 0:
            return WO.at[(y + 4 - d) % 4, many, 0]
        return WO.at[many, (x + 4 - d) % 4, 1]

    def wa_copy(half, way, part):
        ref = w_piece(half, 0, part)
        return remote(ref, ref, wasem.at[half, way, part], warsem.at[half, way, part], along(half, way))

    def wa_relay(half, way):
        ref = w_piece(half, 1 if way == 0 else 3, way)
        return remote(ref, ref, wasem.at[half, way, 2], warsem.at[half, way, 2], along(half, way))

    def wb_copy(half, way, part):
        ref = w_chunk(half, 0, part)
        return remote(ref, ref, wbsem.at[half, way, part], wbrsem.at[half, way, part], along(1 - half, way))

    def wb_relay(half, way):
        ref = w_chunk(half, 3, way)
        return remote(ref, ref, wbsem.at[half, way, 2], wbrsem.at[half, way, 2], along(1 - half, 1))

    every = [(half, way) for way in (0, 1) for half in (0, 1)]

    def w_a1():
        w_placed()
        for part in (0, 1):
            for half, way in every:
                wa_copy(half, way, part ^ way).start()

    def w_a2():
        for half, way in every:
            wa_copy(half, way, way).wait_recv()
            wa_relay(half, way).start()

    def w_b1():
        for half, way in every:
            wa_copy(half, way, 1 - way).wait_recv()
            wa_relay(half, way).wait_recv()
        for part in (0, 1):
            for half, way in every:
                wb_copy(half, way, part ^ way).start()

    def w_b2():
        for part in (1, 0):
            for half in (0, 1):
                wb_copy(half, 1, part).wait_recv()
                wb_relay(half, part).start()

    def w_done():
        for half, way in every:
            wb_copy(half, 0, way).wait_recv()
        for half, way in every:
            wb_relay(half, way).wait_recv()

    step_a1(0)

    def x_copy(i, by):
        src = N.at[pl.ds(pl.multiple_of(768 + i * LNB, LNB), LNB)]
        dst = N.at[pl.ds(pl.multiple_of(zh * 384 + i * LNB, LNB), LNB)]
        k = 0 if by == 1 else 1
        return remote(src, dst, xsem.at[k, i], xrsem.at[zh, i], place(x, y, z + by, 1 - c))

    def ln_rows(i, s):
        span = jnp.where(swapped, zh, (i * LNB) // 384)

        def body(j, carry):
            r = pl.multiple_of(j * 16, 16)
            hid = lstage[s, pl.ds(r, 16), :].astype(F32) + cstage[s, pl.ds(r, 16), :].astype(F32)
            cen = hid - jnp.mean(hid, axis=-1, keepdims=True)
            var = jnp.mean(cen * cen, axis=-1, keepdims=True)
            nrm = cen * lax.rsqrt(var + 1e-6) * (1.0 + mods[span, 1:2, :]) + mods[span, 0:1, :]
            N[pl.ds(pl.multiple_of(out0 + i * LNB + r, 16), 16), :] = nrm.astype(BF)
            return carry

        lax.fori_loop(0, LNB // 16, body, 0, unroll=True)

    def ln_step(i, carry):
        s = i % 2

        @pl.when(i + 1 < n_chunks)
        def _():
            for cp in stage(i + 1, 1 - s):
                cp.start()

        for cp in stage(i, s):
            cp.wait()
        ln_rows(i, s)

        @pl.when(swapped & (i > 0))
        def _():
            x_copy(i - 1, 1).start()
            x_copy(i - 1, 3).start()

        return carry

    part_chunks = n_chunks // 6
    weave = {0: (step_a1, 1), 1: (step_a2, 0), 2: (step_a1, 2), 3: (step_a2, 1), 4: (step_b1, 0), 5: (step_a2, 2)}

    def ln_weave(i, carry):
        ln_step(i, carry)
        for seg, (fn, m) in weave.items():
            @pl.when(i == (seg + 1) * part_chunks - 1)
            def _(fn=fn, m=m):
                fn(m)

        return carry

    lax.fori_loop(0, n_chunks, ln_weave, 0)

    @pl.when(swapped)
    def _():
        x_copy(384 // LNB - 1, 1).start()
        x_copy(384 // LNB - 1, 3).start()

    def rows_of(r):
        return [pl.ds(pl.multiple_of(s * 384 + r * (TILE // 2), TILE // 2), TILE // 2) for s in (0, 1)]

    def lhs(r, k0, kn):
        return jnp.concatenate([N[rs, pl.ds(k0, kn)] for rs in rows_of(r)], axis=0)

    def put(m, r, cols, val, first):
        for s, rs in enumerate(rows_of(r)):
            part = val[s * (TILE // 2):(s + 1) * (TILE // 2)]
            if first:
                acc[m, rs, cols] = part
            else:
                acc[m, rs, cols] += part

    def x_dot(m, d, r, first):
        yy = (y + 4 - d) % 4
        w = W[m, yy, :, :, :, 0:XCS[m]].reshape(1280, XCS[m])
        v = jnp.dot(lhs(r, pl.multiple_of(yy * 1280, 1280), 1280), w, preferred_element_type=F32)
        put(m, r, slice(0, XCS[m]), v, first)

    def y_dot(m, xp, r, first):
        v = None
        for yy in range(4):
            w = W[m, yy, pl.ds(2 * xp, 2), :, :, XCS[m]:640].reshape(640, 640 - XCS[m])
            t = jnp.dot(lhs(r, pl.multiple_of(yy * 1280 + xp * 640, 640), 640), w, preferred_element_type=F32)
            v = t if v is None else v + t
        put(m, r, slice(XCS[m], 640), v, first)

    def shared(m, half, d):
        f_copy(m, half, d).wait_recv()

    def rows_ready(r):
        @pl.when(swapped)
        def _():
            for span in (0, 1):
                lo = r * (TILE // 2) // LNB
                hi = -(-(r + 1) * (TILE // 2) // LNB)
                prev = -(-r * (TILE // 2) // LNB)
                for i in range(max(lo, prev), hi):
                    src = N.at[pl.ds(768 + i * LNB, LNB)]
                    dst = N.at[pl.ds(span * 384 + i * LNB, LNB)]
                    remote(src, dst, xsem.at[0, i], xrsem.at[span, i], partner).wait_recv()

    def row_sq(m, dst):
        for t in range(6):
            v = acc[m, pl.ds(t * 128, 128), :].astype(BF).astype(F32)
            s = jnp.sum(v * v, axis=-1, keepdims=True)
            wide = jnp.broadcast_to(s, (128, 128))
            sq[dst, :, pl.ds(t * 128, 128)] = jnp.transpose(wide)[0:8, :]

    def s_copy(k, d):
        return remote(
            sq.at[k], sqr.at[k, d - 1], ssem.at[k, d - 1], srsem.at[k, d - 1], place(x, y, z + d, c)
        )

    def normalize(k, m, gain, out):
        for d in (1, 2, 3):
            s_copy(k, d).wait_recv()
        tot = sq[k] + sqr[k, 0] + sqr[k, 1] + sqr[k, 2]
        scale = lax.rsqrt(tot / 2560.0 + 1e-6)
        for t in range(6):
            col = jnp.transpose(jnp.broadcast_to(scale[0:1, t * 128:(t + 1) * 128], (128, 128)))
            rs = pl.ds(t * 128, 128)
            v = acc[m, rs, :].astype(BF).astype(F32)
            out[rs, :] = (v * col[:, 0:1] * biaso[gain:gain + 1, 0:640]).astype(BF)

    def steps(m, kinds, rlo, rhi, fresh):
        for kind, d in kinds:
            if fresh:
                if kind == "x":
                    shared(m, 0, d)
                elif d == 0:
                    for dd in (0, 1, 3):
                        shared(m, 1, dd)
                else:
                    shared(m, 1, 2)

            def body(r, carry, kind=kind, d=d):
                if kind == "x":
                    x_dot(m, d, r, d == 0)
                else:
                    y_dot(m, x // 2 if d == 0 else 1 - x // 2, r, d == 0)
                return carry

            lax.fori_loop(rlo, rhi, body, 0)

    early = (("x", 0), ("x", 1), ("x", 3), ("y", 0))
    late = (("x", 2), ("y", 1))

    def head_cols(i):
        return pl.ds(pl.multiple_of(i * HD, HD), HD)

    def k_copy(t, i, dev):
        return remote(
            (ko, vo)[t].at[:, head_cols(i)], (pko, pvo)[t].at[:, head_cols(i)], ksem.at[t, i], krsem.at[t, i], dev
        )

    step_b2(0)
    step_b1(1)
    step_f(0)
    step_f2(0)
    step_b2(1)
    step_b1(2)
    rows_ready(0)
    rows_ready(1)
    steps(0, early + late, 0, 2, True)
    step_f(1)
    step_f2(1)
    w_place()
    steps(1, early + late, 0, 2, True)
    step_b2(2)
    step_f(2)
    rows_ready(2)
    steps(0, early + late, 2, 3, False)
    steps(1, early + late, 2, 3, False)
    w_a1()
    rows_ready(3)
    steps(0, early + late, 3, 4, False)

    @pl.when(swapped)
    def _():
        remote(bias, biaso, bisem, birsem, swap_dev).wait()

    @pl.when(jnp.logical_not(swapped))
    def _():
        pltpu.make_async_copy(bias, biaso, bisem).wait()

    row_sq(0, 0)
    for d in (1, 3, 2):
        s_copy(0, d).start()
    steps(1, early + late, 3, 4, False)
    for t in range(6):
        rs = pl.ds(t * 128, 128)
        vo[rs, :] = acc[1, rs, :].astype(BF)
    normalize(0, 0, 17, ko)
    step_f2(2)
    w_a2()

    for i in range(5):
        @pl.when(c == 0)
        def _():
            for t in (0, 1):
                k_copy(t, i, partner).start()

        @pl.when(c == 1)
        def _():
            for t in (0, 1):
                k_copy(t, i, nxt).start()

    steps(2, early, 0, 4, True)
    w_b1()
    steps(2, late, 0, 4, True)
    row_sq(2, 1)
    for d in (1, 3, 2):
        s_copy(1, d).start()
    normalize(1, 2, 16, qo)

    cols = pl.ds(pl.multiple_of(h * 1280, 1280), 1280)
    resid = (
        pltpu.make_async_copy(lat.at[:, cols], N.at[pl.ds(0, 768), pl.ds(0, 1280)], lsem.at[1]),
        pltpu.make_async_copy(ctl.at[:, cols], N.at[pl.ds(0, 768), pl.ds(1280, 1280)], lsem.at[2]),
    )
    for cp in resid:
        cp.start()

    mine = c == zl
    fold = HD ** -0.5 * 1.4426950408889634

    def attend_head(i, s):
        cs = head_cols(i)

        ones = jnp.ones((384, HD), BF)
        halves = (pl.ds(0, 384), pl.ds(384, 384))
        srcs = (
            ((pko, pvo, 0), (pko, pvo, 1), (ko, vo, 0)),
            ((pko, pvo, 1), (ko, vo, 0), (ko, vo, 1)),
        )
        for b, (kr, _, part) in enumerate(srcs[s]):
            acc[b, halves[s], 0:384] = lax.dot_general(
                qo[halves[s], cs], kr[halves[part], cs], (((1,), (1,)), ((), ())), preferred_element_type=F32
            )
        if True:
            bs = [biaso[8 * s:8 * s + 1, b * 384:b * 384 + 1] for b in range(3)]
            for t in range(6):
                rs = pl.ds(s * 384 + t * 64, 64)
                blocks = [acc[b, rs, 0:384] for b in range(3)]
                wide = None
                for sc, bv in zip(blocks, bs):
                    w = jnp.maximum(jnp.maximum(sc[:, 0:128], sc[:, 128:256]), sc[:, 256:384]) + bv
                    wide = w if wide is None else jnp.maximum(wide, w)
                top = jnp.max(wide, axis=-1, keepdims=True)
                for b in range(3):
                    ex = jnp.exp2((blocks[b] - (top - bs[b])) * fold)
                    EX[rs, b * 384:(b + 1) * 384] = ex.astype(BF)
            o = None
            for b, (_, vr, part) in enumerate(srcs[s]):
                vv = jnp.concatenate([vr[halves[part], cs], ones], axis=1)
                pv = jnp.dot(EX[halves[s], b * 384:(b + 1) * 384], vv, preferred_element_type=F32)
                o = pv if o is None else o + pv
            qo[halves[s], cs] = (o[:, 0:HD] * (1.0 / o[:, HD:HD + 1])).astype(BF)

    def at_view(ref, u):
        i, sp = u
        return ref.at[pl.ds(sp * 384, 384), head_cols(i)]

    def t_copy(d, u):
        i, sp = u
        return remote(
            at_view(qo, u), at_view(AT.at[z], u), tsem.at[d - 1, sp, i], trsem.at[d - 1, sp, i], place(x, y, z + d, c)
        )

    def own_copy(u):
        i, sp = u
        return pltpu.make_async_copy(at_view(qo, u), at_view(AT.at[z], u), osem.at[sp, i])

    def g_own(u):
        i, sp = u
        return remote(at_view(qo, u), at_view(AT.at[z], u), gsem.at[z, sp, i], grsem.at[z, sp, i], partner)

    def g_copy(g, u):
        i, sp = u
        ref = at_view(AT.at[g], u)
        return remote(ref, ref, gsem.at[g, sp, i], grsem.at[g, sp, i], partner)

    def send_unit(u):
        @pl.when(mine)
        def _():
            t_copy(2, u).start()
            own_copy(u).start()
            g_own(u).start()

        @pl.when(jnp.logical_not(mine))
        def _():
            t_copy(1, u).start()
            t_copy(3, u).start()

    def gather_span(sp):
        @pl.when(mine)
        def _():
            for i in range(5):
                for d in (1, 3, 2):
                    t_copy(d, (i, sp)).wait_recv()
                    g_copy((z + 4 - d) % 4, (i, sp)).start()
            for i in range(5):
                own_copy((i, sp)).wait()

        @pl.when(jnp.logical_not(mine))
        def _():
            for i in range(5):
                for g in range(4):
                    g_copy(g, (i, sp)).wait_recv()

    for sp in (1, 0):
        def one_head(i, carry, sp=sp):
            if sp == 1:
                for t in (0, 1):
                    k_copy(t, i, partner).wait_recv()
            attend_head(i, sp)
            send_unit((i, sp))
            return carry

        lax.fori_loop(0, 5, one_head, 0)
        if sp == 1:
            w_b2()
    for cp in resid:
        cp.wait()

    def project_rows(r, n):
        rs = pl.ds(r, n)
        tot = None
        for g in range(4):
            t = lax.dot_general(
                AT[g, rs, :], WO[g].reshape(1280, 640), (((1,), (1,)), ((), ())), preferred_element_type=F32
            ).astype(BF).astype(F32)
            tot = t if tot is None else tot + t
        hid = N[rs, 0:1280].astype(F32) + N[rs, 1280:2560].astype(F32)
        return hid + mods[r // 384, 2:3, cols] * tot

    def h_copy(t):
        rs = pl.ds(t * 192, 192)
        return remote(shout.at[rs], shin.at[rs], hsem.at[t], hrsem.at[t], after)

    gather_span(1)
    w_done()
    for t in (0, 1):
        shout[pl.ds(t * 192, 192), :] = project_rows(384 + t * 192, 192).astype(BF)
        if t:
            h_copy(0).start()
    gather_span(0)
    h_copy(1).start()
    for t in (0, 1):
        out[pl.ds(t * 192, 192), :] = project_rows(t * 192, 192)
    for t in (0, 1):
        h_copy(t).wait_recv()

    for t in (0, 1):
        h_copy(t).wait_send()
    for t in (0, 1):
        for i in range(5):
            k_copy(t, i, partner).wait_send()
    for k in (0, 1):
        for d in (1, 2, 3):
            s_copy(k, d).wait_send()
    for m in range(3):
        for half in (0, 1):
            for way in (0, 1):
                for part in (0, 1):
                    a_copy(m, half, way, part).wait_send()
                    b_copy(m, half, way, part).wait_send()
                a_relay(m, half, way).wait_send()
                b_relay(m, half, way).wait_send()
            for d in range(4):
                f_copy(m, half, d).wait_send()

    @pl.when(swapped)
    def _():
        for i in range(384 // LNB):
            x_copy(i, 1).wait_send()
            x_copy(i, 3).wait_send()

    for half, way in every:
        for part in (0, 1):
            wa_copy(half, way, part).wait_send()
            wb_copy(half, way, part).wait_send()
        wa_relay(half, way).wait_send()
        wb_relay(half, way).wait_send()

    @pl.when(y != h)
    def _():
        for t in (0, 1):
            remote(wo, spot, rsem.at[t], rrsem.at[zl], swapdev(t)).wait_send()

    @pl.when(y == h)
    def _():
        remote(wo, spot, rsem.at[0], rrsem.at[zl], swapdev(1 - zl)).wait_send()

    units = [(i, sp) for sp in (1, 0) for i in range(5)]

    @pl.when(mine)
    def _():
        for u in units:
            t_copy(2, u).wait_send()
            g_own(u).wait_send()
            for d in (1, 2, 3):
                g_copy((z + 4 - d) % 4, u).wait_send()

    @pl.when(jnp.logical_not(mine))
    def _():
        for u in units:
            t_copy(1, u).wait_send()
            t_copy(3, u).wait_send()


def block(lat, ctl, mods, wk, wv, wq, bias, wo):
    any_ = pl.BlockSpec(memory_space=pl.ANY)
    vm = pl.BlockSpec(memory_space=pltpu.VMEM)
    D = pltpu.SemaphoreType.DMA
    rows = pltpu.VMEM((768, 640), BF)
    stage2 = D((3, 2, 2, 3))
    return pl.pallas_call(
        block_kernel,
        out_shape=[jax.ShapeDtypeStruct((384, 1280), F32), jax.ShapeDtypeStruct((384, 1280), BF)],
        in_specs=[any_, any_, vm, any_, any_, any_, any_, any_],
        out_specs=[vm, vm],
        scratch_shapes=[
            pltpu.VMEM((3, 4, 4, 2, 160, 640), BF),
            pltpu.VMEM((1152, 5120), BF),
            pltpu.VMEM((2, LNB, 5120), BF),
            pltpu.VMEM((2, LNB, 5120), BF),
            pltpu.VMEM((3, 768, 640), F32),
            pltpu.VMEM((2, 8, 768), F32),
            pltpu.VMEM((2, 3, 8, 768), F32),
            rows, rows, rows, rows, rows,
            pltpu.VMEM((24, 1152), F32),
            pltpu.VMEM((4, 4, 2, 160, 640), BF),
            pltpu.VMEM((4, 768, 640), BF),
            pltpu.VMEM((384, 1280), BF),
            pltpu.VMEM((768, 1152), BF),
            D((2, 2)), D((3,)), D((3,)),
            stage2, stage2, stage2, stage2, D((3, 2, 4)), D((3, 2, 4)),
            D((2, 384 // LNB)), D((2, 384 // LNB)), D((2, 3)), D((2, 3)), D((2, 5)), D((2, 5)), D, D,
            D((2,)), D((2,)), D((2, 2, 3)), D((2, 2, 3)), D((2, 2, 3)), D((2, 2, 3)),
            D((3, 2, 5)), D((3, 2, 5)), D((4, 2, 5)), D((4, 2, 5)), D((3,)), D((2,)), D((2,)), D((2, 5)),
        ],
        compiler_params=pltpu.CompilerParams(
            collective_id=0, has_side_effects=True, vmem_limit_bytes=67043328
        ),
        name="block",
    )(lat, ctl, mods, wk, wv, wq, bias, wo)


def set_up_kernel(levels, mask, table, qg, kg, mods, aux):
    i = pl.program_id(0)
    row = levels[i] % 8
    for k in range(3):
        mods[0, k:k + 1, :] = table[k, pl.ds(row, 1), :]
    first = lax.axis_index("queue") * 2

    @pl.when(i == 0)
    def _():
        aux[...] = jnp.zeros_like(aux)
        aux[16:17, 0:640] = qg[...].reshape(1, 640)
        aux[17:18, 0:640] = kg[...].reshape(1, 640)
        for s in (0, 1):
            far = (mask[s, 0] == 1) & (first + s >= 2)
            near = (mask[s, 1] == 1) & (first + s >= 1)
            aux[8 * s:8 * s + 8, 0:384] = jnp.full((8, 384), jnp.where(far, 0.0, -1e30), F32)
            aux[8 * s:8 * s + 8, 384:768] = jnp.full((8, 384), jnp.where(near, 0.0, -1e30), F32)


def set_up(levels, window_mask, modulation, q_gain, k_gain):
    gain = pl.BlockSpec((640,), lambda i, levels, mask: (0,))
    return pl.pallas_call(
        set_up_kernel,
        grid_spec=pltpu.PrefetchScalarGridSpec(
            num_scalar_prefetch=2,
            grid=(2,),
            in_specs=[
                pl.BlockSpec((3, 8, 5120), lambda i, levels, mask: (0, levels[i] // 8, 0)),
                gain,
                gain,
            ],
            out_specs=[
                pl.BlockSpec((1, 3, 5120), lambda i, levels, mask: (i, 0, 0)),
                pl.BlockSpec((24, 1152), lambda i, levels, mask: (0, 0)),
            ],
        ),
        out_shape=[jax.ShapeDtypeStruct((2, 3, 5120), F32), jax.ShapeDtypeStruct((24, 1152), F32)],
        name="set_up",
    )(levels, window_mask, jnp.transpose(modulation, (1, 0, 2)), q_gain, k_gain)


def shards(latents, control, levels, window_mask, modulation, w_query, w_key, w_value, w_out, q_gain, k_gain):
    lat = latents.reshape(768, 5120)
    ctl = control.reshape(768, 5120)
    mods, aux = set_up(levels, window_mask, modulation, q_gain, k_gain)
    even, odd = block(lat, ctl, mods, w_key, w_value, w_query, aux, w_out.T)
    return jnp.stack([odd.astype(F32), even])


def solution(mesh):
    placed = (
        P("queue", None, None),
        P("queue", None, None),
        P("queue"),
        P("queue", None),
        P(),
        P("queue", "head"),
        P("queue", "head"),
        P("queue", "head"),
        P("head", "queue"),
        P("head"),
        P("head"),
    )
    return jax.shard_map(
        shards, mesh=mesh, in_specs=placed, out_specs=P("queue", None, "head"), check_vma=False
    )
```

profile of v0, /device:TPU:0, one launch (start us, length us, event | category | flops | bytes accessed | tf_op | source)
XLA Modules:
  0.0 162.6 jit_solution(2941502487652992475)
XLA Ops:
  0.0 2.6 %set_up.1 = (f32[2,3,5120]{2,1,0:T(4,128)}, f32[24,1152]{1,0:T(8,128)}) custom-call(s32[2]{0:T(128)} %levels.1, s32[2,2]{1,0:T(2,128)} %mask.1, f32[3,64,5120]{2,1,0:T(8,128)} %bitcast.10, f32[640]{0:T(1024)} %qg.1, f32[640]{0:T(1024)} %kg.1), custom_call_target="tpu_custom_call" | custom-call | tf_op jit(solution)/shard_map/set_up/pallas_call | solution.py:776
  2.6 155.9 %block.1 = (f32[384,1280]{1,0:T(8,128)}, bf16[384,1280]{1,0:T(8,128)(2,1)}) custom-call(bf16[768,5120]{1,0:T(8,128)(2,1)} %bitcast.8, bf16[768,5120]{1,0:T(8,128)(2,1)} %bitcast.9, f32[2,3,5120]{2,1,0:T(4,128)} %get-tuple-element.9.mods, bf16[160,640]{1,0:T(8,128)(2,1)} %wk.1, bf16[160,640]{1,0:T(8,128)(2,1)} %wv.1, bf16[160,640]{1,0:T(8,128)(2,1)} %wq.1, ...), custom_call_target="tpu_custom_call" | custom-call | tf_op jit(solution)/shard_map/block/pallas_call | solution.py:723
  158.6 0.0 copy-start
  158.6 1.5 bitcast_convert_fusion
  160.0 0.4 copy-done
  160.4 2.2 %pad_maximum_fusion = f32[2,384,1280]{2,1,0:T(8,128)} fusion(f32[1,384,1280]{2,1,0:T(8,128)S(1)} %bitcast.11, f32[1,384,1280]{2,1,0:T(8,128)S(1)} %bitcast_convert_fusion), kind=kLoop, calls=%fused_computation | loop fusion | flops 983040 | bytes 7864320 | tf_op jit(solution)/shard_map/stack | solution.py:801
Async XLA Ops:
  158.6 1.8 %copy-start = (f32[384,1280]{1,0:T(8,128)S(1)}, f32[384,1280]{1,0:T(8,128)}, u32[]{:S(2)}) copy-start(f32[384,1280]{1,0:T(8,128)} %get-tuple-element.12) | copy-start | bytes 5898244
where the time goes:
time: 165 us; the launch traced here: 163 us
  Pallas kernels  159 us (96%)
  other arithmetic  3.65 us (2%)
    pallas_call x1, Pallas kernels, block(): pl.pallas_call(block_kernel, out_shape=[jax.ShapeDtypeStruct((384, 1280),...  156 us
    another operation x2, other arithmetic, shards(): return jnp.stack([odd.astype(F32), even])  3.65 us

commit v1 on v0

--- a/solution.py
+++ b/solution.py
@@ -597,19 +597,19 @@
             t_copy(1, u).start()
             t_copy(3, u).start()
 
-    def gather_span(sp):
+    def gather_span(sp, heads=range(5)):
         @pl.when(mine)
         def _():
-            for i in range(5):
+            for i in heads:
                 for d in (1, 3, 2):
                     t_copy(d, (i, sp)).wait_recv()
                     g_copy((z + 4 - d) % 4, (i, sp)).start()
-            for i in range(5):
+            for i in heads:
                 own_copy((i, sp)).wait()
 
         @pl.when(jnp.logical_not(mine))
         def _():
-            for i in range(5):
+            for i in heads:
                 for g in range(4):
                     g_copy(g, (i, sp)).wait_recv()
 
@@ -649,8 +649,9 @@
         shout[pl.ds(t * 192, 192), :] = project_rows(384 + t * 192, 192).astype(BF)
         if t:
             h_copy(0).start()
-    gather_span(0)
+    gather_span(0, range(1))
     h_copy(1).start()
+    gather_span(0, range(1, 5))
     for t in (0, 1):
         out[pl.ds(t * 192, 192), :] = project_rows(t * 192, 192)
     for t in (0, 1):

time: 165 us -> 165 us (level)
  no operation moved by 1% of the time
where the time goes in v1:
time: 165 us; the launch traced here: 163 us
  Pallas kernels  159 us (96%)
  other arithmetic  3.65 us (2%)
    pallas_call x1, Pallas kernels, block(): pl.pallas_call(block_kernel, out_shape=[jax.ShapeDtypeStruct((384, 1280),...  156 us
    another operation x2, other arithmetic, shards(): return jnp.stack([odd.astype(F32), even])  3.65 us

profile of v1, /device:TPU:0, one launch (start us, length us, event | category | flops | bytes accessed | tf_op | source)
XLA Modules:
  0.0 162.7 jit_solution(11893363870404151609)
XLA Ops:
  0.0 2.6 %set_up.1 = (f32[2,3,5120]{2,1,0:T(4,128)}, f32[24,1152]{1,0:T(8,128)}) custom-call(s32[2]{0:T(128)} %levels.1, s32[2,2]{1,0:T(2,128)} %mask.1, f32[3,64,5120]{2,1,0:T(8,128)} %bitcast.10, f32[640]{0:T(1024)} %qg.1, f32[640]{0:T(1024)} %kg.1), custom_call_target="tpu_custom_call" | custom-call | tf_op jit(solution)/shard_map/set_up/pallas_call | solution.py:777
  2.6 156.0 %block.1 = (f32[384,1280]{1,0:T(8,128)}, bf16[384,1280]{1,0:T(8,128)(2,1)}) custom-call(bf16[768,5120]{1,0:T(8,128)(2,1)} %bitcast.8, bf16[768,5120]{1,0:T(8,128)(2,1)} %bitcast.9, f32[2,3,5120]{2,1,0:T(4,128)} %get-tuple-element.9.mods, bf16[160,640]{1,0:T(8,128)(2,1)} %wk.1, bf16[160,640]{1,0:T(8,128)(2,1)} %wv.1, bf16[160,640]{1,0:T(8,128)(2,1)} %wq.1, ...), custom_call_target="tpu_custom_call" | custom-call | tf_op jit(solution)/shard_map/block/pallas_call | solution.py:724
  158.7 0.0 copy-start
  158.7 1.5 bitcast_convert_fusion
  160.1 0.4 copy-done
  160.5 2.2 %pad_maximum_fusion = f32[2,384,1280]{2,1,0:T(8,128)} fusion(f32[1,384,1280]{2,1,0:T(8,128)S(1)} %bitcast.11, f32[1,384,1280]{2,1,0:T(8,128)S(1)} %bitcast_convert_fusion), kind=kLoop, calls=%fused_computation | loop fusion | flops 983040 | bytes 7864320 | tf_op jit(solution)/shard_map/stack | solution.py:802
Async XLA Ops:
  158.7 1.8 %copy-start = (f32[384,1280]{1,0:T(8,128)S(1)}, f32[384,1280]{1,0:T(8,128)}, u32[]{:S(2)}) copy-start(f32[384,1280]{1,0:T(8,128)} %get-tuple-element.12) | copy-start | bytes 5898244
